TPU v7x, 32 devices: a whole 2x2x4 slice. The times are simulated.
32 devices in a mesh: panel: 2 (over y), dom: 4 (over z), blk: 2 (over x), dir: 2 (over core).
Axes of the slice: x: 2, y: 2, z: 4, core: 2. Of those that a mesh axis runs over, the one named last changes fastest.
Arguments:
- panel_vectors: bfloat16 [3072, 2048], P('dom', ('panel', 'blk')), parts along dimension 1, may hold values from -6 to 6
- force_blocks: float32 [16, 9, 1024], P(None, None, 'dom'), may hold values from -1 to 1
- bond_vectors: float32 [2, 16, 1024], P('dir', None, 'dom'), may hold values from -4 to 4
- neighbours: int32 [16, 1024], P(None, 'dom'), may hold values from 0 to 511
- boundary_low: int32 [512], P('dom'), may hold values from 0 to 255
- boundary_high: int32 [512], P('dom'), may hold values from 0 to 255
Outputs:
- coupling: float32 [2, 2048, 1024], P('dir', ('panel', 'dom'), 'blk'), parts along dimension 1
There are 2 independent parts, one for each index of `panel`. A program takes and returns all parts, laid end to end along the dimension named above; an argument that names none is the same for every part. Nothing has to cross between parts.
Inputs may be any that keep to these rules, and one draw needn't show every extreme that they name: `neighbours`: an entry below 256 names an atom of the same domain; from 256 to 383 the listed boundary atoms of the domain below; from 384 on those of the domain above. `boundary_low`: local atom numbers within the domain that owns the block; repeats may occur. `boundary_high`: local atom numbers within the domain that owns the block; repeats may occur.
All inputs are finite; a program needn't handle non-finite values.
Results may differ from a plain program's by a relative error of at most 0.0029.
Values may be sent and summed in bfloat16 or wider, within the bound.
A program may use at most 64 MiB of HBM per device.

v0:
```python
import jax
import jax.numpy as jnp
from jax import lax
from jax.sharding import PartitionSpec as P

K = 16


def from_behind(value, axis, by):
    length = lax.axis_size(axis)
    return lax.ppermute(value, axis, [(i, (i + by) % length) for i in range(length)])


def per_device(panel_vectors, force_blocks, bond_vectors, neighbours, boundary_low, boundary_high):
    rows, cols = panel_vectors.shape
    atoms = rows // 3
    own = panel_vectors.reshape(atoms, 3, cols)
    send_low = own[boundary_low]
    send_high = own[boundary_high]
    below = from_behind(send_high, "dom", 1)
    above = from_behind(send_low, "dom", -1)
    extended = jnp.concatenate([own, below, above], axis=0)
    weights = force_blocks * bond_vectors[0][:, None, :]
    flux = jnp.zeros((atoms, 3, cols), jnp.float32)
    for k in range(K):
        gathered = extended[neighbours[k]]
        blocks = weights[k].reshape(3, 3, atoms).transpose(2, 0, 1)
        flux = flux + jnp.sum(blocks[:, :, :, None] * gathered[:, None, :, :], axis=2)
    flux_rows = flux.astype(jnp.bfloat16).reshape(rows, cols)
    partial_sum = jnp.dot(
        lax.all_gather(panel_vectors, "blk", axis=1, tiled=True).T,
        flux_rows,
        preferred_element_type=jnp.float32,
    )
    domains = lax.axis_size("dom")
    scale = (3.0 * atoms * domains) ** (-0.5)
    result = lax.psum_scatter(partial_sum, "dom", scatter_dimension=0, tiled=True)
    return (result * scale)[None, :, :]


def solution(mesh):
    in_specs = (
        P("dom", ("panel", "blk")),
        P(None, None, "dom"),
        P("dir", None, "dom"),
        P(None, "dom"),
        P("dom"),
        P("dom"),
    )
    out_specs = P("dir", ("panel", "dom"), "blk")
    return jax.shard_map(
        per_device, mesh=mesh, in_specs=in_specs, out_specs=out_specs, check_vma=False
    )
```

profile of v0, /device:TPU:0, one launch (start us, length us, event | category | flops | bytes accessed | tf_op | source)
XLA Modules:
  0.0 185.0 jit_solution(13326271073689447377)
XLA Ops:
  7.3 2.5 %reshape.553 = bf16[256,3,512]{2,1,0:T(4,128)(2,1)S(1)} reshape(bf16[768,512]{1,0:T(8,128)(2,1)} %param.6) | data formatting | bytes 1572864 | tf_op jit(solution)/shard_map/reshape | solution.py:17
  9.9 1.8 gather_fusion
  11.7 3.0 %collective-permute-start = (bf16[128,3,512]{2,1,0:T(4,128)(2,1)}, bf16[128,3,512]{2,1,0:T(4,128)(2,1)}, u32[]{:S(2)}, u32[]{:S(2)}) collective-permute-start(bf16[128,3,512]{2,1,0:T(4,128)(2,1)} %gather_fusion), channel_id=1, source_target_pairs={{0,4},{4,8},{8,12},{12,0},{1,5},{5,9},{9,13},{13,1},{2,6},{6,10},{... | collective-permute-start | bytes 1179656 | tf_op jit(solution)/shard_map/ppermute | solution.py:11
  14.7 1.8 gather_fusion.1
  16.5 2.0 %collective-permute-start.1 = (bf16[128,3,512]{2,1,0:T(4,128)(2,1)}, bf16[128,3,512]{2,1,0:T(4,128)(2,1)}, u32[]{:S(2)}, u32[]{:S(2)}) collective-permute-start(bf16[128,3,512]{2,1,0:T(4,128)(2,1)} %gather_fusion.1), channel_id=1, source_target_pairs={{0,12},{4,0},{8,4},{12,8},{1,13},{5,1},{9,5},{13,9},{2,14},{6,2},{... | collective-permute-start | bytes 1179656 | tf_op jit(solution)/shard_map/ppermute | solution.py:11
  19.7 10.1 %collective-permute-done = bf16[128,3,512]{2,1,0:T(4,128)(2,1)} collective-permute-done((bf16[128,3,512]{2,1,0:T(4,128)(2,1)}, bf16[128,3,512]{2,1,0:T(4,128)(2,1)}, u32[]{:S(2)}, u32[]{:S(2)}) %collective-permute-start) | collective-permute-done | bytes 393248 | tf_op jit(solution)/shard_map/ppermute | solution.py:11
  31.1 9.1 %collective-permute-done.1 = bf16[128,3,512]{2,1,0:T(4,128)(2,1)} collective-permute-done((bf16[128,3,512]{2,1,0:T(4,128)(2,1)}, bf16[128,3,512]{2,1,0:T(4,128)(2,1)}, u32[]{:S(2)}, u32[]{:S(2)}) %collective-permute-start.1) | collective-permute-done | bytes 393248 | tf_op jit(solution)/shard_map/ppermute | solution.py:11
  56.2 1.5 gather_fusion.3
  62.1 1.5 gather_fusion.15
  65.1 1.7 gather_fusion.14
  89.2 1.6 multiply_reduce_fusion.11
  90.8 1.6 multiply_reduce_fusion.12
  95.6 1.6 multiply_reduce_fusion.15
  97.2 1.5 multiply_reduce_fusion.2
  98.8 1.6 multiply_reduce_fusion.3
  100.4 1.6 multiply_reduce_fusion.4
  102.0 1.7 multiply_reduce_fusion.5
  103.7 1.6 multiply_reduce_fusion.6
  105.3 1.5 multiply_reduce_fusion.7
  108.4 1.6 multiply_reduce_fusion.9
  114.3 10.8 %add_convert_fusion = bf16[256,3,512]{2,0,1:T(8,128)(2,1)} fusion(f32[256,3,512]{2,0,1:T(8,128)} %multiply_reduce_fusion, f32[256,3,512]{2,0,1:T(8,128)S(1)} %copy-done.9, f32[256,3,512]{2,0,1:T(8,128)} %multiply_reduce_fusion.2, f32[256,3,512]{2,0,1:T(8,128)} %multiply_reduce_fusion.3, f32[256,3,512]{2,0,1:T(8,128)} %multiply_reduce_fusion.4, ...), kind=kLoop, calls=%fused_computation.35 | loop fusion | flops 6291456 | bytes 25952256 | tf_op jit(solution)/shard_map/convert_element_type | solution.py:29
  125.1 1.8 copy.77
  127.7 3.7 %convolution_bitcast_fusion = f32[1024,512]{0,1:T(8,128)} fusion(bf16[768,512]{1,0:T(8,128)(2,1)S(1)} %reshape.711, bf16[768,1024]{1,0:T(8,128)(2,1)} %all-gather.2.cloned.1.call-done), kind=kOutput, calls=%fused_computation.34 | convolution fusion | flops 805306368 | bytes 4456448 | tf_op jit(solution)/shard_map/dot_general | solution.py:30
  131.4 44.7 %reduce-scatter.2.cloned.1.call-done = f32[256,512]{0,1:T(8,128)} async-done(((f32[1024,512]{0,1:T(8,128)}), f32[256,512]{0,1:T(8,128)}) %reduce-scatter.2.cloned.1.call-update) | async-done | bytes 524304 | tf_op jit(solution)/shard_map/reduce_scatter | solution.py:37
  (118 shorter events, 59.1 us)
Async XLA Ops:
  6.5 3.3 %copy-start.19 = (s32[128]{0:T(128)S(1)}, s32[128]{0:T(128)}, u32[]{:S(2)}) copy-start(s32[128]{0:T(128)} %param.10) | copy-start | bytes 1540
  6.5 3.3 %copy-start.20 = (s32[128]{0:T(128)S(1)}, s32[128]{0:T(128)}, u32[]{:S(2)}) copy-start(s32[128]{0:T(128)} %param.11) | copy-start | bytes 1540
  6.5 121.2 %all-gather.2.cloned.1.call-start = ((), (), s32[]{:S(2)}) async-start(), calls=%async_computation.1 | async-start | bytes 2359296 | tf_op jit(solution)/shard_map/all_gather | solution.py:31
  7.3 11.3 %copy-start.18 = (s32[16,256]{1,0:T(8,128)S(1)}, s32[16,256]{1,0:T(8,128)}, u32[]{:S(2)}) copy-start(s32[16,256]{1,0:T(8,128)} %param.9) | copy-start | bytes 49156
  7.3 11.3 %copy-start.16 = (f32[16,9,256]{2,0,1:T(8,128)S(1)}, f32[16,9,256]{2,0,1:T(8,128)}, u32[]{:S(2)}) copy-start(f32[16,9,256]{2,0,1:T(8,128)} %param.7) | copy-start | bytes 442372
  7.3 11.3 %copy-start.17 = (f32[1,16,256]{2,1,0:T(8,128)S(1)}, f32[1,16,256]{2,1,0:T(8,128)}, u32[]{:S(2)}) copy-start(f32[1,16,256]{2,1,0:T(8,128)} %param.8) | copy-start | bytes 49156
  7.3 168.8 %reduce-scatter.2.cloned.1.call-start = ((), (), s32[]{:S(2)}) async-start(), calls=%async_computation.2 | async-start | bytes 2621440 | tf_op jit(solution)/shard_map/reduce_scatter | solution.py:37
  11.7 18.2 %collective-permute-start = (bf16[128,3,512]{2,1,0:T(4,128)(2,1)}, bf16[128,3,512]{2,1,0:T(4,128)(2,1)}, u32[]{:S(2)}, u32[]{:S(2)}) collective-permute-start(bf16[128,3,512]{2,1,0:T(4,128)(2,1)} %gather_fusion), channel_id=1, source_target_pairs={{0,4},{4,8},{8,12},{12,0},{1,5},{5,9},{9,13},{13,1},{2,6},{6,10},{... | collective-permute-start | bytes 1179656 | tf_op jit(solution)/shard_map/ppermute | solution.py:11
  16.5 23.7 %collective-permute-start.1 = (bf16[128,3,512]{2,1,0:T(4,128)(2,1)}, bf16[128,3,512]{2,1,0:T(4,128)(2,1)}, u32[]{:S(2)}, u32[]{:S(2)}) collective-permute-start(bf16[128,3,512]{2,1,0:T(4,128)(2,1)} %gather_fusion.1), channel_id=1, source_target_pairs={{0,12},{4,0},{8,4},{12,8},{1,13},{5,1},{9,5},{13,9},{2,14},{6,2},{... | collective-permute-start | bytes 1179656 | tf_op jit(solution)/shard_map/ppermute | solution.py:11
  86.0 1.6 copy-start.1
  87.6 1.6 copy-start.2
  89.2 1.6 copy-start.3
  90.8 1.6 copy-start.4
  92.4 1.6 copy-start.5
  94.0 1.6 copy-start.6
  95.6 1.6 copy-start.7
  97.2 1.6 copy-start.8
  98.8 1.6 copy-start.10
  100.4 1.6 copy-start.12
  102.0 1.8 copy-start.13
  103.7 1.6 copy-start.14
  105.3 1.6 copy-start.15
  111.9 1.6 copy-start.9
  111.9 2.4 %copy-start.11 = (f32[256,3,512]{2,0,1:T(8,128)S(1)}, f32[256,3,512]{2,0,1:T(8,128)}, u32[]{:S(2)}) copy-start(f32[256,3,512]{2,0,1:T(8,128)} %multiply_reduce_fusion.10) | copy-start | bytes 4718596
  (1 other events, 1.4 us)
Sparse Core Ops, SparseCore 0:
  8.9 29.8 all-gather.1
  131.6 44.5 reduce-scatter.1
where the time goes:
time: 186 us; the launch traced here: 185 us
  waiting for transfers between devices  64.7 us (35%)
  other arithmetic  57.4 us (31%)
  local copies, waits for them, and re-layouts  40.3 us (22%)
  between operations  13.9 us (7%)
  starting transfers between devices  5.09 us (3%)
  matrix products  3.71 us (2%)
    reduce_scatter x1, waiting for transfers between devices, per_device(): lax.psum_scatter(partial_sum, 'dom', scatter_dimension=0, tiled=True)  44.7 us
    reduce_sum x16, other arithmetic, per_device(): jnp.sum(blocks[:, :, :, None] * gathered[:, None, :, :], axis=2)  25 us
    gather x16, local copies, waits for them, and re-layouts, per_device(): gathered = extended[neighbours[k]]  24.7 us
    convert_element_type x16, other arithmetic, per_device(): blocks[:, :, :, None] * gathered[:, None, :, :]  20.4 us
    ppermute x2, waiting for transfers between devices, from_behind(): lax.ppermute(value, axis, [(i, (i + by) % length) for i in range(length)])  19.2 us
    convert_element_type x1, other arithmetic, per_device(): flux_rows = flux.astype(jnp.bfloat16).reshape(rows, cols)  10.8 us
    ppermute x2, starting transfers between devices, from_behind(): lax.ppermute(value, axis, [(i, (i + by) % length) for i in range(length)])  5.05 us
    unnamed x44, local copies, waits for them, and re-layouts  4.28 us
  transfers between devices with their start and end apart: 4, of which 3 were waited for; matrix products, arithmetic and copies ran while one was open for 50% of the time, Pallas kernels for 0%

commit v1 on v0

v1 whole, which is shorter than its diff:
```python
import functools

import jax
import jax.numpy as jnp
from jax import lax
from jax.experimental import pallas as pl
from jax.experimental.pallas import tpu as pltpu
from jax.sharding import PartitionSpec as P

MESH = pl.DeviceIdType.MESH
BF16 = jnp.bfloat16
F32 = jnp.float32


def one_hot(hits):
    return jnp.where(hits, 1.0, 0.0).astype(BF16)


def dot(a, b):
    return jnp.dot(a, b, preferred_element_type=F32)


def kernel(n, nblk, v_ref, force_ref, bond_ref, nbr_ref, low_ref, high_ref, out_ref,
           vt, vx, hs, ht, w, st_hi, st_lo, flux, ft, part, su, ru, sd, rd,
           h_send, h_recv, hf_send, hf_recv, x_send, x_recv, xf_send, xf_recv,
           u_send, u_recv, d_send, d_recv):
    me = lax.axis_index("dom")
    blk = lax.axis_index("blk")
    core = lax.axis_index("dir")
    rows, cols = v_ref.shape
    atoms = rows // 3
    half = cols // 2
    bnd = low_ref.shape[1]
    steps = nbr_ref.shape[0]
    tile = out_ref.shape[0]
    up, down = lax.rem(me + 1, n), lax.rem(me + n - 1, n)
    peers = [{"dom": up}, {"dom": down}, {"dir": 1 - core}]
    peers += [{"blk": lax.rem(blk + o, nblk)} for o in range(1, nblk)]

    barrier = pltpu.get_barrier_semaphore()
    for peer in peers:
        pl.semaphore_signal(barrier, inc=1, device_id=peer, device_id_type=MESH)

    vt[...] = v_ref[...].T
    mine = vt[pl.ds(pl.multiple_of(core * half, half), half), :]
    atom_row = lax.broadcasted_iota(jnp.int32, (rows, bnd), 0)
    for side, list_ref in ((0, high_ref), (1, low_ref)):
        for b in range(3):
            pick = one_hot(atom_row == 3 * list_ref[...] + b)
            hs[side, b] = dot(mine, pick).astype(BF16)
    pl.semaphore_wait(barrier, len(peers))

    halo = [
        pltpu.make_async_remote_copy(
            src_ref=hs.at[side], dst_ref=ht.at[side, core],
            send_sem=h_send.at[side], recv_sem=h_recv.at[side],
            device_id={"dom": up if side == 0 else down}, device_id_type=MESH)
        for side in range(2)
    ]
    for copy in halo:
        copy.start()

    row_of = lax.broadcasted_iota(jnp.int32, (rows, atoms), 0)
    atom_of = lax.broadcasted_iota(jnp.int32, (rows, atoms), 1)
    for a in range(3):
        pick = one_hot(row_of == 3 * atom_of + a)
        for h in range(2):
            vx[blk, h, :, a * atoms:(a + 1) * atoms] = dot(vt[h * half:(h + 1) * half, :], pick).astype(BF16)

    tiles = [
        pltpu.make_async_remote_copy(
            src_ref=vx.at[blk, core], dst_ref=vx.at[blk, core],
            send_sem=x_send.at[o - 1], recv_sem=x_recv.at[o - 1],
            device_id={"blk": lax.rem(blk + o, nblk)}, device_id_type=MESH)
        for o in range(1, nblk)
    ]
    for copy in tiles:
        copy.start()

    for k in range(steps):
        w[k] = force_ref[k] * bond_ref[0, k:k + 1, :]
    group = 16
    lanes = min(atoms, 256)

    def build(t, carry):
        j0 = pl.multiple_of(t * group, group)
        region = t // (atoms // group)
        base = pl.multiple_of(region * rows + (j0 - region * atoms), group)
        for i0 in range(0, atoms, lanes):
            js = lax.broadcasted_iota(jnp.int32, (group, lanes), 0) + j0
            total = [jnp.zeros((group, lanes), F32) for _ in range(9)]
            for k in range(steps):
                hit = js == nbr_ref[k:k + 1, i0:i0 + lanes]
                for q in range(9):
                    total[q] = total[q] + jnp.where(hit, w[k, q:q + 1, i0:i0 + lanes], 0.0)
            for a in range(3):
                for b in range(3):
                    value = total[3 * a + b]
                    high = value.astype(BF16)
                    at = (pl.ds(pl.multiple_of(base + b * atoms, group), group),
                          slice(a * atoms + i0, a * atoms + i0 + lanes))
                    st_hi[at] = high
                    st_lo[at] = (value - high.astype(F32)).astype(BF16)
        return carry

    lax.fori_loop(0, (atoms + 2 * bnd) // group, build, 0)

    for h in range(2):
        own = vx[blk, h]
        flux[h] = dot(own, st_hi[:rows, :]) + dot(own, st_lo[:rows, :])

    halo_on = []
    for side in range(2):
        halo[side].wait_recv()
        copy = pltpu.make_async_remote_copy(
            src_ref=ht.at[side, core], dst_ref=ht.at[side, core],
            send_sem=hf_send.at[side], recv_sem=hf_recv.at[side],
            device_id={"dir": 1 - core}, device_id_type=MESH)
        copy.start()
        halo_on.append(copy)
    tiles_on = []
    for o in range(1, nblk):
        tiles[o - 1].wait_recv()
        source = lax.rem(blk + nblk - o, nblk)
        copy = pltpu.make_async_remote_copy(
            src_ref=vx.at[source, core], dst_ref=vx.at[source, core],
            send_sem=xf_send.at[o - 1], recv_sem=xf_recv.at[o - 1],
            device_id={"dir": 1 - core}, device_id_type=MESH)
        copy.start()
        tiles_on.append(copy)
    for copy in halo_on:
        copy.wait_recv()
    for h in range(2):
        outer = jnp.concatenate([ht[side, h, b] for b in range(3) for side in range(2)], axis=1)
        total = flux[h] + dot(outer, st_hi[rows:, :]) + dot(outer, st_lo[rows:, :])
        ft[h * half:(h + 1) * half, :] = total.astype(BF16)

    for copy in tiles_on:
        copy.wait_recv()
    for b in range(nblk):
        for h in range(2):
            first = b * cols + h * half
            part[first:first + half, :] = lax.dot_general(
                vx[b, h], ft[...], (((1,), (1,)), ((), ())), preferred_element_type=F32)

    def term(e):
        return part[pl.ds(pl.multiple_of(e * tile, tile), tile), :]

    def hop(e, out, into, send, recv, target):
        return pltpu.make_async_remote_copy(
            src_ref=out.at[e], dst_ref=into.at[e], send_sem=send.at[e], recv_sem=recv.at[e],
            device_id={"dom": target}, device_id_type=MESH)

    def rising(e):
        return hop(e, su, ru, u_send, u_recv, up)

    def falling(e):
        return hop(e, sd, rd, d_send, d_recv, down)

    for t in range(n - 1):
        for first, away, make, out, into in (
            (me, n - 1 - (t - me), rising, su, ru),
            (n - 1 - me, t - (n - 1 - me), falling, sd, rd),
        ):
            @pl.when(first <= t)
            def _(first=first, e=away, make=make, out=out, into=into):
                @pl.when(first == 0)
                def _():
                    out[e] = term(e).astype(out.dtype)

                @pl.when(first > 0)
                def _():
                    make(e).wait_recv()
                    out[e] = (term(e) + into[e].astype(F32)).astype(out.dtype)

                make(e).start()

    out_ref[...] = term(me)

    @pl.when(me > 0)
    def _():
        rising(me).wait_recv()
        out_ref[...] += ru[me].astype(F32)

    @pl.when(me < n - 1)
    def _():
        falling(me).wait_recv()
        out_ref[...] += rd[me].astype(F32)

    for t in range(n - 1):
        @pl.when(me <= t)
        def _(t=t):
            rising(n - 1 - (t - me)).wait_send()

        @pl.when(n - 1 - me <= t)
        def _(t=t):
            falling(t - (n - 1 - me)).wait_send()

    for copy in halo + halo_on + tiles + tiles_on:
        copy.wait_send()


def per_device(n, nblk, panel_vectors, force_blocks, bond_vectors, neighbours, boundary_low, boundary_high):
    rows, cols = panel_vectors.shape
    atoms = rows // 3
    half = cols // 2
    bnd = boundary_low.shape[0]
    steps = neighbours.shape[0]
    tile = nblk * cols // n
    wire = BF16 if n <= 4 else F32
    vmem = pl.BlockSpec(memory_space=pltpu.VMEM)
    line = pltpu.VMEM((n, tile, cols), wire)
    dma = pltpu.SemaphoreType.DMA
    result = pl.pallas_call(
        functools.partial(kernel, n, nblk),
        out_shape=jax.ShapeDtypeStruct((tile, cols), F32),
        in_specs=[vmem] * 6,
        out_specs=vmem,
        scratch_shapes=[
            pltpu.VMEM((cols, rows), BF16),
            pltpu.VMEM((nblk, 2, half, rows), BF16),
            pltpu.VMEM((2, 3, half, bnd), BF16),
            pltpu.VMEM((2, 2, 3, half, bnd), BF16),
            pltpu.VMEM((steps, 9, atoms), F32),
            pltpu.VMEM((2 * rows, rows), BF16),
            pltpu.VMEM((2 * rows, rows), BF16),
            pltpu.VMEM((2, half, rows), F32),
            pltpu.VMEM((cols, rows), BF16),
            pltpu.VMEM((nblk * cols, cols), F32),
            line, line, line, line,
            dma((2,)), dma((2,)), dma((2,)), dma((2,)),
            dma((nblk - 1,)), dma((nblk - 1,)), dma((nblk - 1,)), dma((nblk - 1,)),
            dma((n,)), dma((n,)), dma((n,)), dma((n,)),
        ],
        compiler_params=pltpu.CompilerParams(
            collective_id=0, has_side_effects=True, vmem_limit_bytes=48 * 1024 * 1024
        ),
    )(panel_vectors, force_blocks, bond_vectors, neighbours,
      boundary_low.reshape(1, bnd), boundary_high.reshape(1, bnd))
    scale = (3.0 * atoms * n) ** (-0.5)
    return (result * scale)[None, :, :]


def solution(mesh):
    in_specs = (
        P("dom", ("panel", "blk")),
        P(None, None, "dom"),
        P("dir", None, "dom"),
        P(None, "dom"),
        P("dom"),
        P("dom"),
    )
    out_specs = P("dir", ("panel", "dom"), "blk")
    return jax.shard_map(
        functools.partial(per_device, mesh.shape["dom"], mesh.shape["blk"]),
        mesh=mesh, in_specs=in_specs, out_specs=out_specs, check_vma=False
    )
```

time: 186 us -> 44.7 us (0.24)
  waiting for transfers between devices: 64.7 us -> 0 us
  other arithmetic: 57.4 us -> 0.84 us
  Pallas kernels: 0 us -> 41.4 us
  local copies, waits for them, and re-layouts: 40.3 us -> 2.2 us
  between operations: 13.9 us -> 0.05 us
  starting transfers between devices: 5.09 us -> 0 us
  matrix products: 3.71 us -> 0 us
    reduce_scatter x1 -> x0, waiting for transfers between devices: 44.7 us -> none  [per_device(): lax.psum_scatter(partial_sum, 'dom', scatter_dimension=0, tiled=True)]
    pallas_call x0 -> x1, Pallas kernels: none -> 41.4 us  [per_device(): pl.pallas_call(functools.partial(kernel, n, nblk), out_shape=jax.ShapeDty...]
    convert_element_type x17 -> x0, other arithmetic: 31.2 us -> none  [the longest x16 20.4 us: per_device(): blocks[:, :, :, None] * gathered[:, None, :, :]]
    gather x18 -> x0, local copies, waits for them, and re-layouts: 28.3 us -> none  [the longest x16 24.7 us: per_device(): gathered = extended[neighbours[k]]]
    reduce_sum x16 -> x0, other arithmetic: 25 us -> none  [per_device(): jnp.sum(blocks[:, :, :, None] * gathered[:, None, :, :], axis=2)]
    ppermute x2 -> x0, waiting for transfers between devices: 19.2 us -> none  [from_behind(): lax.ppermute(value, axis, [(i, (i + by) % length) for i in range(length)])]
    ppermute x2 -> x0, starting transfers between devices: 5.05 us -> none  [from_behind(): lax.ppermute(value, axis, [(i, (i + by) % length) for i in range(length)])]
    dot_general x1 -> x0, matrix products: 3.71 us -> none  [per_device(): jnp.dot(lax.all_gather(panel_vectors, 'blk', axis=1, tiled=True).T, flux_...]
  transfers between devices with their start and end apart: 4 -> 0, of which waited for: 3 -> 0; matrix products, arithmetic and copies ran while one was open for 50% -> 0% of each run, Pallas kernels for 0% -> 0%
where the time goes in v1:
time: 44.7 us; the launch traced here: 44.5 us
  Pallas kernels  41.4 us (93%)
  local copies, waits for them, and re-layouts  2.2 us (5%)
  other arithmetic  0.84 us (2%)
    pallas_call x1, Pallas kernels, per_device(): pl.pallas_call(functools.partial(kernel, n, nblk), out_shape=jax.ShapeDty...  41.4 us
    unnamed x11, local copies, waits for them, and re-layouts  2.2 us

profile of v1, /device:TPU:0, one launch (start us, length us, event | category | flops | bytes accessed | tf_op | source)
XLA Modules:
  0.0 44.5 jit_solution(14671044994278426473)
XLA Ops:
  0.0 0.0 copy-start.1
  0.0 0.0 copy-start.2
  0.0 0.0 copy-start.3
  0.0 0.0 copy-start.4
  0.0 1.1 %copy.7.force_ref = f32[16,9,256]{2,1,0:T(8,128)S(1)} copy(f32[16,9,256]{2,0,1:T(8,128)} %param.7) | data formatting | bytes 294912 | tf_op args[1]
  1.1 0.0 copy-done.1
  1.1 0.0 copy-done.2
  1.1 0.0 copy-done.3
  1.1 0.0 copy-done.4
  1.1 0.0 copy-start
  1.1 1.1 %copy-done = bf16[768,512]{1,0:T(8,128)(2,1)S(1)} copy-done((bf16[768,512]{1,0:T(8,128)(2,1)S(1)}, bf16[768,512]{1,0:T(8,128)(2,1)}, u32[]{:S(2)}) %copy-start) | copy-done | bytes 786456
  2.2 41.4 %shard_map.64 = f32[256,512]{1,0:T(8,128)S(1)} custom-call(bf16[768,512]{1,0:T(8,128)(2,1)S(1)} %copy-done, f32[16,9,256]{2,1,0:T(8,128)S(1)} %copy.7.force_ref, f32[1,16,256]{2,1,0:T(8,128)S(1)} %copy-done.1, s32[16,256]{1,0:T(8,128)S(1)} %copy-done.2, s32[1,128]{1,0:T(1,128)S(1)} %bitcast.4, s32[1,128]{1,0:T(1,128)S(1)} %bitcast.5), custom_call_target="tpu_custom_call" | custom-call | tf_op jit(solution)/shard_map/pallas_call | solution.py:214
  43.7 0.8 %multiply_bitcast_fusion = f32[1,256,512]{2,1,0:T(8,128)} fusion(f32[256,512]{1,0:T(8,128)S(1)} %shard_map.64), kind=kLoop, calls=%fused_computation | loop fusion | flops 131072 | bytes 1048576 | tf_op jit(solution)/shard_map/broadcast_in_dim | solution.py:241
Async XLA Ops:
  0.0 1.1 %copy-start.1 = (f32[1,16,256]{2,1,0:T(8,128)S(1)}, f32[1,16,256]{2,1,0:T(8,128)}, u32[]{:S(2)}) copy-start(f32[1,16,256]{2,1,0:T(8,128)} %bond_ref.1) | copy-start | bytes 49156
  0.0 1.1 %copy-start.2 = (s32[16,256]{1,0:T(8,128)S(1)}, s32[16,256]{1,0:T(8,128)}, u32[]{:S(2)}) copy-start(s32[16,256]{1,0:T(8,128)} %nbr_ref.1) | copy-start | bytes 49156
  0.0 1.1 %copy-start.3 = (s32[128]{0:T(128)S(1)}, s32[128]{0:T(128)}, u32[]{:S(2)}) copy-start(s32[128]{0:T(128)} %param.10) | copy-start | bytes 1540
  0.0 1.1 %copy-start.4 = (s32[128]{0:T(128)S(1)}, s32[128]{0:T(128)}, u32[]{:S(2)}) copy-start(s32[128]{0:T(128)} %param.11) | copy-start | bytes 1540
  1.1 1.1 %copy-start = (bf16[768,512]{1,0:T(8,128)(2,1)S(1)}, bf16[768,512]{1,0:T(8,128)(2,1)}, u32[]{:S(2)}) copy-start(bf16[768,512]{1,0:T(8,128)(2,1)} %v_ref.1) | copy-start | bytes 2359300

commit v2 on v1

v2 whole, which is shorter than its diff:
```python
import functools

import jax
import jax.numpy as jnp
from jax import lax
from jax.experimental import pallas as pl
from jax.experimental.pallas import tpu as pltpu
from jax.sharding import PartitionSpec as P

MESH = pl.DeviceIdType.MESH
BF16 = jnp.bfloat16
F32 = jnp.float32


def one_hot(hits):
    return jnp.where(hits, 1.0, 0.0).astype(BF16)


def dot(a, b):
    return jnp.dot(a, b, preferred_element_type=F32)


def kernel(n, nblk, pieces, v_ref, force_ref, bond_ref, nbr_ref, low_ref, high_ref, out_ref,
           vt, vx, hs, ht, w, wd, st_hi, st_lo, flux, part, su, ru, sd, rd,
           h_send, h_recv, hf_send, hf_recv, x_send, x_recv, xf_send, xf_recv,
           u_send, u_recv, d_send, d_recv):
    me = lax.axis_index("dom")
    blk = lax.axis_index("blk")
    core = lax.axis_index("dir")
    rows, cols = v_ref.shape
    atoms = rows // 3
    half = cols // 2
    share = half // 2
    bnd = low_ref.shape[1]
    steps = nbr_ref.shape[0]
    tile = out_ref.shape[0]
    piece = tile // pieces
    up, down = lax.rem(me + 1, n), lax.rem(me + n - 1, n)
    peers = [{"dom": up}, {"dom": down}, {"dir": 1 - core}]
    peers += [{"blk": lax.rem(blk + o, nblk)} for o in range(1, nblk)]

    barrier = pltpu.get_barrier_semaphore()
    for peer in peers:
        pl.semaphore_signal(barrier, inc=1, device_id=peer, device_id_type=MESH)

    vt[...] = v_ref[...].T
    mine = jnp.concatenate(
        [vt[pl.ds(pl.multiple_of(h * half + core * share, share), share), :] for h in range(2)], axis=0)
    atom_row = lax.broadcasted_iota(jnp.int32, (rows, bnd), 0)
    for side, list_ref in ((0, high_ref), (1, low_ref)):
        for b in range(3):
            pick = one_hot(atom_row == 3 * list_ref[...] + b)
            rows_out = dot(mine, pick).astype(BF16)
            for h in range(2):
                hs[side, h, b] = rows_out[h * share:(h + 1) * share]
    pl.semaphore_wait(barrier, len(peers))

    halo = {
        (side, h): pltpu.make_async_remote_copy(
            src_ref=hs.at[side, h], dst_ref=ht.at[side, h, core],
            send_sem=h_send.at[2 * side + h], recv_sem=h_recv.at[2 * side + h],
            device_id={"dom": up if side == 0 else down}, device_id_type=MESH)
        for h in range(2) for side in range(2)
    }
    for copy in halo.values():
        copy.start()

    row_of = lax.broadcasted_iota(jnp.int32, (rows, atoms), 0)
    atom_of = lax.broadcasted_iota(jnp.int32, (rows, atoms), 1)
    for a in range(3):
        pick = one_hot(row_of == 3 * atom_of + a)
        for h in range(2):
            vx[blk, h, :, a * atoms:(a + 1) * atoms] = dot(vt[h * half:(h + 1) * half, :], pick).astype(BF16)

    tiles = [
        pltpu.make_async_remote_copy(
            src_ref=vx.at[blk, core], dst_ref=vx.at[blk, core],
            send_sem=x_send.at[o - 1], recv_sem=x_recv.at[o - 1],
            device_id={"blk": lax.rem(blk + o, nblk)}, device_id_type=MESH)
        for o in range(1, nblk)
    ]
    for copy in tiles:
        copy.start()

    for k in range(steps):
        w[k] = force_ref[k] * bond_ref[0, k:k + 1, :]
    for k in range(steps):
        total = w[k]
        name = jnp.broadcast_to(nbr_ref[k:k + 1, :], total.shape)
        for other in range(k):
            total = total + jnp.where(name == nbr_ref[other:other + 1, :], w[other], 0.0)
        wd[k] = total

    group = 16
    lanes = min(atoms, 256)

    def build(t, carry):
        j0 = pl.multiple_of(t * group, group)
        region = t // (atoms // group)
        base = pl.multiple_of(region * rows + (j0 - region * atoms), group)
        for i0 in range(0, atoms, lanes):
            js = lax.broadcasted_iota(jnp.int32, (group, lanes), 0) + j0
            total = [jnp.zeros((group, lanes), F32) for _ in range(9)]
            for k in range(steps):
                hit = js == nbr_ref[k:k + 1, i0:i0 + lanes]
                for q in range(9):
                    total[q] = jnp.where(hit, wd[k, q:q + 1, i0:i0 + lanes], total[q])
            for a in range(3):
                for b in range(3):
                    value = total[3 * a + b]
                    high = value.astype(BF16)
                    at = (pl.ds(pl.multiple_of(base + b * atoms, group), group),
                          slice(a * atoms + i0, a * atoms + i0 + lanes))
                    st_hi[at] = high
                    st_lo[at] = (value - high.astype(F32)).astype(BF16)
        return carry

    lax.fori_loop(0, (atoms + 2 * bnd) // group, build, 0)

    onward = {}
    tiles_on = []

    def pass_halo(h):
        for side in range(2):
            halo[side, h].wait_recv()
            onward[side, h] = pltpu.make_async_remote_copy(
                src_ref=ht.at[side, h, core], dst_ref=ht.at[side, h, core],
                send_sem=hf_send.at[2 * side + h], recv_sem=hf_recv.at[2 * side + h],
                device_id={"dir": 1 - core}, device_id_type=MESH)
            onward[side, h].start()

    def pass_tiles():
        for o in range(1, nblk):
            tiles[o - 1].wait_recv()
            source = lax.rem(blk + nblk - o, nblk)
            copy = pltpu.make_async_remote_copy(
                src_ref=vx.at[source, core], dst_ref=vx.at[source, core],
                send_sem=xf_send.at[o - 1], recv_sem=xf_recv.at[o - 1],
                device_id={"dir": 1 - core}, device_id_type=MESH)
            copy.start()
            tiles_on.append(copy)

    def term(h, e, r):
        return part[h, pl.ds(pl.multiple_of(e * tile + r * piece, piece), piece), :]

    def hop(h, e, r, out, into, send, recv, target):
        cell = (h * n + e) * pieces + r
        here = pl.ds(r * piece, piece)
        return pltpu.make_async_remote_copy(
            src_ref=out.at[h, e, here], dst_ref=into.at[h, e, here],
            send_sem=send.at[cell], recv_sem=recv.at[cell],
            device_id={"dom": target}, device_id_type=MESH)

    def rising(h, e, r):
        return hop(h, e, r, su, ru, u_send, u_recv, up)

    def falling(h, e, r):
        return hop(h, e, r, sd, rd, d_send, d_recv, down)

    def ends(t):
        return ((me, n - 1 - (t - me), rising, su, ru),
                (n - 1 - me, t - (n - 1 - me), falling, sd, rd))

    def own_flux(h):
        own = vx[blk, h]
        flux[h] = dot(own, st_hi[:rows, :]) + dot(own, st_lo[:rows, :])

    def couple(h):
        for side in range(2):
            onward[side, h].wait_recv()
        outer = jnp.concatenate(
            [jnp.concatenate([ht[side, h, c, b] for b in range(3) for side in range(2)], axis=1)
             for c in range(2)], axis=0)
        total = flux[h] + dot(outer, st_hi[rows:, :]) + dot(outer, st_lo[rows:, :])
        return total.astype(BF16)

    def multiply(h, columns):
        part[h] = lax.dot_general(
            vx[...].reshape(nblk * cols, rows), columns, (((1,), (1,)), ((), ())),
            preferred_element_type=F32)

    def emit(h):
        for t in range(n - 1):
            for first, e, make, out, into in ends(t):
                @pl.when(first == 0)
                def _(t=t, e=e, make=make, out=out):
                    for r in range(pieces):
                        out[h, e, r * piece:(r + 1) * piece] = term(h, e, r).astype(out.dtype)
                        make(h, e, r).start()

    own_flux(0)
    pass_halo(0)
    pass_tiles()
    own_flux(1)
    columns = couple(0)
    for copy in tiles_on:
        copy.wait_recv()
    multiply(0, columns)
    emit(0)
    pass_halo(1)
    multiply(1, couple(1))
    emit(1)

    for h in range(2):
        for t in range(1, n - 1):
            for r in range(pieces):
                for first, e, make, out, into in ends(t):
                    @pl.when((first > 0) & (first <= t))
                    def _(r=r, e=e, make=make, out=out, into=into):
                        here = slice(r * piece, (r + 1) * piece)
                        make(h, e, r).wait_recv()
                        out[h, e, here] = (term(h, e, r) + into[h, e, here].astype(F32)).astype(out.dtype)
                        make(h, e, r).start()

    for h in range(2):
        for r in range(pieces):
            here = slice(r * piece, (r + 1) * piece)
            there = slice(h * half, (h + 1) * half)

            @pl.when(me == 0)
            def _():
                falling(h, me, r).wait_recv()
                out_ref[here, there] = term(h, me, r) + rd[h, me, here].astype(F32)

            @pl.when(me == n - 1)
            def _():
                rising(h, me, r).wait_recv()
                out_ref[here, there] = term(h, me, r) + ru[h, me, here].astype(F32)

            @pl.when((me > 0) & (me < n - 1))
            def _():
                rising(h, me, r).wait_recv()
                falling(h, me, r).wait_recv()
                out_ref[here, there] = (
                    term(h, me, r) + ru[h, me, here].astype(F32) + rd[h, me, here].astype(F32))

    for h in range(2):
        for t in range(n - 1):
            for first, e, make, out, into in ends(t):
                @pl.when(first <= t)
                def _(e=e, make=make):
                    for r in range(pieces):
                        make(h, e, r).wait_send()

    for copy in [*halo.values(), *onward.values(), *tiles, *tiles_on]:
        copy.wait_send()


def per_device(n, nblk, panel_vectors, force_blocks, bond_vectors, neighbours, boundary_low, boundary_high):
    rows, cols = panel_vectors.shape
    atoms = rows // 3
    half = cols // 2
    bnd = boundary_low.shape[0]
    steps = neighbours.shape[0]
    tile = nblk * cols // n
    wire = BF16 if n <= 4 else F32
    vmem = pl.BlockSpec(memory_space=pltpu.VMEM)
    pieces = 2
    line = pltpu.VMEM((2, n, tile, half), wire)
    hops = pltpu.SemaphoreType.DMA((2 * n * pieces,))
    dma = pltpu.SemaphoreType.DMA
    result = pl.pallas_call(
        functools.partial(kernel, n, nblk, pieces),
        out_shape=jax.ShapeDtypeStruct((tile, cols), F32),
        in_specs=[vmem] * 6,
        out_specs=vmem,
        scratch_shapes=[
            pltpu.VMEM((cols, rows), BF16),
            pltpu.VMEM((nblk, 2, half, rows), BF16),
            pltpu.VMEM((2, 2, 3, half // 2, bnd), BF16),
            pltpu.VMEM((2, 2, 2, 3, half // 2, bnd), BF16),
            pltpu.VMEM((steps, 9, atoms), F32),
            pltpu.VMEM((steps, 9, atoms), F32),
            pltpu.VMEM((2 * rows, rows), BF16),
            pltpu.VMEM((2 * rows, rows), BF16),
            pltpu.VMEM((2, half, rows), F32),
            pltpu.VMEM((2, nblk * cols, half), F32),
            line, line, line, line,
            dma((4,)), dma((4,)), dma((4,)), dma((4,)),
            dma((nblk - 1,)), dma((nblk - 1,)), dma((nblk - 1,)), dma((nblk - 1,)),
            hops, hops, hops, hops,
        ],
        compiler_params=pltpu.CompilerParams(
            collective_id=0, has_side_effects=True, vmem_limit_bytes=48 * 1024 * 1024
        ),
    )(panel_vectors, force_blocks, bond_vectors, neighbours,
      boundary_low.reshape(1, bnd), boundary_high.reshape(1, bnd))
    scale = (3.0 * atoms * n) ** (-0.5)
    return (result * scale)[None, :, :]


def solution(mesh):
    in_specs = (
        P("dom", ("panel", "blk")),
        P(None, None, "dom"),
        P("dir", None, "dom"),
        P(None, "dom"),
        P("dom"),
        P("dom"),
    )
    out_specs = P("dir", ("panel", "dom"), "blk")
    return jax.shard_map(
        functools.partial(per_device, mesh.shape["dom"], mesh.shape["blk"]),
        mesh=mesh, in_specs=in_specs, out_specs=out_specs, check_vma=False
    )
```

time: 44.7 us -> 43.1 us (0.964)
  Pallas kernels: 41.4 us -> 39.8 us
    pallas_call x1, Pallas kernels: 41.4 us -> 39.8 us  [per_device(): pl.pallas_call(functools.partial(kernel, n, nblk, pieces), out_shape=jax....]
where the time goes in v2:
time: 43.1 us; the launch traced here: 42.9 us
  Pallas kernels  39.8 us (92%)
  local copies, waits for them, and re-layouts  2.2 us (5%)
  other arithmetic  0.84 us (2%)
    pallas_call x1, Pallas kernels, per_device(): pl.pallas_call(functools.partial(kernel, n, nblk, pieces), out_shape=jax....  39.8 us
    unnamed x11, local copies, waits for them, and re-layouts  2.2 us

profile of v2, /device:TPU:0, one launch (start us, length us, event | category | flops | bytes accessed | tf_op | source)
XLA Modules:
  0.0 42.9 jit_solution(17104082820355839547)
XLA Ops:
  0.0 0.0 copy-start.1
  0.0 0.0 copy-start.2
  0.0 0.0 copy-start.3
  0.0 0.0 copy-start.4
  0.0 1.1 %copy.7.force_ref = f32[16,9,256]{2,1,0:T(8,128)S(1)} copy(f32[16,9,256]{2,0,1:T(8,128)} %param.7) | data formatting | bytes 294912 | tf_op args[1]
  1.1 0.0 copy-done.1
  1.1 0.0 copy-done.2
  1.1 0.0 copy-done.3
  1.1 0.0 copy-done.4
  1.1 0.0 copy-start
  1.1 1.1 %copy-done = bf16[768,512]{1,0:T(8,128)(2,1)S(1)} copy-done((bf16[768,512]{1,0:T(8,128)(2,1)S(1)}, bf16[768,512]{1,0:T(8,128)(2,1)}, u32[]{:S(2)}) %copy-start) | copy-done | bytes 786456
  2.2 39.8 %shard_map.64 = f32[256,512]{1,0:T(8,128)S(1)} custom-call(bf16[768,512]{1,0:T(8,128)(2,1)S(1)} %copy-done, f32[16,9,256]{2,1,0:T(8,128)S(1)} %copy.7.force_ref, f32[1,16,256]{2,1,0:T(8,128)S(1)} %copy-done.1, s32[16,256]{1,0:T(8,128)S(1)} %copy-done.2, s32[1,128]{1,0:T(1,128)S(1)} %bitcast.4, s32[1,128]{1,0:T(1,128)S(1)} %bitcast.5), custom_call_target="tpu_custom_call" | custom-call | tf_op jit(solution)/shard_map/pallas_call | solution.py:262
  42.1 0.8 %multiply_bitcast_fusion = f32[1,256,512]{2,1,0:T(8,128)} fusion(f32[256,512]{1,0:T(8,128)S(1)} %shard_map.64), kind=kLoop, calls=%fused_computation | loop fusion | flops 131072 | bytes 1048576 | tf_op jit(solution)/shard_map/broadcast_in_dim | solution.py:289
Async XLA Ops:
  0.0 1.1 %copy-start.1 = (f32[1,16,256]{2,1,0:T(8,128)S(1)}, f32[1,16,256]{2,1,0:T(8,128)}, u32[]{:S(2)}) copy-start(f32[1,16,256]{2,1,0:T(8,128)} %bond_ref.1) | copy-start | bytes 49156
  0.0 1.1 %copy-start.2 = (s32[16,256]{1,0:T(8,128)S(1)}, s32[16,256]{1,0:T(8,128)}, u32[]{:S(2)}) copy-start(s32[16,256]{1,0:T(8,128)} %nbr_ref.1) | copy-start | bytes 49156
  0.0 1.1 %copy-start.3 = (s32[128]{0:T(128)S(1)}, s32[128]{0:T(128)}, u32[]{:S(2)}) copy-start(s32[128]{0:T(128)} %param.10) | copy-start | bytes 1540
  0.0 1.1 %copy-start.4 = (s32[128]{0:T(128)S(1)}, s32[128]{0:T(128)}, u32[]{:S(2)}) copy-start(s32[128]{0:T(128)} %param.11) | copy-start | bytes 1540
  1.1 1.1 %copy-start = (bf16[768,512]{1,0:T(8,128)(2,1)S(1)}, bf16[768,512]{1,0:T(8,128)(2,1)}, u32[]{:S(2)}) copy-start(bf16[768,512]{1,0:T(8,128)(2,1)} %v_ref.1) | copy-start | bytes 2359300

commit v3 on v2

--- a/solution.py
+++ b/solution.py
@@ -21,8 +21,8 @@
 
 
 def kernel(n, nblk, pieces, v_ref, force_ref, bond_ref, nbr_ref, low_ref, high_ref, out_ref,
-           vt, vx, hs, ht, w, wd, st_hi, st_lo, flux, part, su, ru, sd, rd,
-           h_send, h_recv, hf_send, hf_recv, x_send, x_recv, xf_send, xf_recv,
+           vbuf, vx, vp, pt, hs, ht, w, wd, st_hi, st_lo, flux, part, su, ru, sd, rd,
+           v_sem, h_send, h_recv, hf_send, hf_recv, x_send, x_recv, xf_send, xf_recv,
            u_send, u_recv, d_send, d_recv):
     me = lax.axis_index("dom")
     blk = lax.axis_index("blk")
@@ -39,13 +39,30 @@
     peers = [{"dom": up}, {"dom": down}, {"dir": 1 - core}]
     peers += [{"blk": lax.rem(blk + o, nblk)} for o in range(1, nblk)]
 
+    fetch = pltpu.make_async_copy(v_ref, vbuf, v_sem)
+    fetch.start()
     barrier = pltpu.get_barrier_semaphore()
     for peer in peers:
         pl.semaphore_signal(barrier, inc=1, device_id=peer, device_id_type=MESH)
 
-    vt[...] = v_ref[...].T
+    fetch.wait()
+    turned = vbuf[...].T
+    for h in range(2):
+        vx[blk, h] = turned[h * half:(h + 1) * half]
+    pl.semaphore_wait(barrier, len(peers))
+
+    tiles = [
+        pltpu.make_async_remote_copy(
+            src_ref=vx.at[blk, core], dst_ref=vx.at[blk, core],
+            send_sem=x_send.at[o - 1], recv_sem=x_recv.at[o - 1],
+            device_id={"blk": lax.rem(blk + o, nblk)}, device_id_type=MESH)
+        for o in range(1, nblk)
+    ]
+    for copy in tiles:
+        copy.start()
+
     mine = jnp.concatenate(
-        [vt[pl.ds(pl.multiple_of(h * half + core * share, share), share), :] for h in range(2)], axis=0)
+        [vx[blk, h, pl.ds(pl.multiple_of(core * share, share), share), :] for h in range(2)], axis=0)
     atom_row = lax.broadcasted_iota(jnp.int32, (rows, bnd), 0)
     for side, list_ref in ((0, high_ref), (1, low_ref)):
         for b in range(3):
@@ -53,7 +70,6 @@
             rows_out = dot(mine, pick).astype(BF16)
             for h in range(2):
                 hs[side, h, b] = rows_out[h * share:(h + 1) * share]
-    pl.semaphore_wait(barrier, len(peers))
 
     halo = {
         (side, h): pltpu.make_async_remote_copy(
@@ -70,17 +86,11 @@
     for a in range(3):
         pick = one_hot(row_of == 3 * atom_of + a)
         for h in range(2):
-            vx[blk, h, :, a * atoms:(a + 1) * atoms] = dot(vt[h * half:(h + 1) * half, :], pick).astype(BF16)
-
-    tiles = [
-        pltpu.make_async_remote_copy(
-            src_ref=vx.at[blk, core], dst_ref=vx.at[blk, core],
-            send_sem=x_send.at[o - 1], recv_sem=x_recv.at[o - 1],
-            device_id={"blk": lax.rem(blk + o, nblk)}, device_id_type=MESH)
-        for o in range(1, nblk)
-    ]
-    for copy in tiles:
-        copy.start()
+            vp[h, :, a * atoms:(a + 1) * atoms] = dot(vx[blk, h], pick).astype(BF16)
+    atom_of = lax.broadcasted_iota(jnp.int32, (atoms, rows), 0)
+    row_of = lax.broadcasted_iota(jnp.int32, (atoms, rows), 1)
+    for a in range(3):
+        pt[a * atoms:(a + 1) * atoms, :] = one_hot(row_of == 3 * atom_of + a)
 
     for k in range(steps):
         w[k] = force_ref[k] * bond_ref[0, k:k + 1, :]
@@ -162,7 +172,7 @@
                 (n - 1 - me, t - (n - 1 - me), falling, sd, rd))
 
     def own_flux(h):
-        own = vx[blk, h]
+        own = vp[h]
         flux[h] = dot(own, st_hi[:rows, :]) + dot(own, st_lo[:rows, :])
 
     def couple(h):
@@ -172,7 +182,7 @@
             [jnp.concatenate([ht[side, h, c, b] for b in range(3) for side in range(2)], axis=1)
              for c in range(2)], axis=0)
         total = flux[h] + dot(outer, st_hi[rows:, :]) + dot(outer, st_lo[rows:, :])
-        return total.astype(BF16)
+        return dot(total.astype(BF16), pt[...]).astype(BF16)
 
     def multiply(h, columns):
         part[h] = lax.dot_general(
@@ -262,11 +272,13 @@
     result = pl.pallas_call(
         functools.partial(kernel, n, nblk, pieces),
         out_shape=jax.ShapeDtypeStruct((tile, cols), F32),
-        in_specs=[vmem] * 6,
+        in_specs=[pl.BlockSpec(memory_space=pl.ANY)] + [vmem] * 5,
         out_specs=vmem,
         scratch_shapes=[
-            pltpu.VMEM((cols, rows), BF16),
+            pltpu.VMEM((rows, cols), BF16),
             pltpu.VMEM((nblk, 2, half, rows), BF16),
+            pltpu.VMEM((2, half, rows), BF16),
+            pltpu.VMEM((rows, rows), BF16),
             pltpu.VMEM((2, 2, 3, half // 2, bnd), BF16),
             pltpu.VMEM((2, 2, 2, 3, half // 2, bnd), BF16),
             pltpu.VMEM((steps, 9, atoms), F32),
@@ -276,7 +288,7 @@
             pltpu.VMEM((2, half, rows), F32),
             pltpu.VMEM((2, nblk * cols, half), F32),
             line, line, line, line,
-            dma((4,)), dma((4,)), dma((4,)), dma((4,)),
+            dma, dma((4,)), dma((4,)), dma((4,)), dma((4,)),
             dma((nblk - 1,)), dma((nblk - 1,)), dma((nblk - 1,)), dma((nblk - 1,)),
             hops, hops, hops, hops,
         ],

time: 43.1 us -> 42.7 us (level)
  no operation moved by 1% of the time
where the time goes in v3:
time: 42.7 us; the launch traced here: 42.5 us
  Pallas kernels  39.4 us (92%)
  local copies, waits for them, and re-layouts  2.2 us (5%)
  other arithmetic  0.84 us (2%)
    pallas_call x1, Pallas kernels, per_device(): pl.pallas_call(functools.partial(kernel, n, nblk, pieces), out_shape=jax....  39.4 us
    unnamed x11, local copies, waits for them, and re-layouts  2.2 us

profile of v3, /device:TPU:0, one launch (start us, length us, event | category | flops | bytes accessed | tf_op | source)
XLA Modules:
  0.0 42.5 jit_solution(10302712169657763885)
XLA Ops:
  0.0 0.0 copy-start.1
  0.0 0.0 copy-start.2
  0.0 0.0 copy-start.3
  0.0 0.0 copy-start.4
  0.0 1.1 %copy.7.force_ref = f32[16,9,256]{2,1,0:T(8,128)S(1)} copy(f32[16,9,256]{2,0,1:T(8,128)} %param.7) | data formatting | bytes 294912 | tf_op args[1]
  1.1 0.0 copy-done.1
  1.1 0.0 copy-done.2
  1.1 0.0 copy-done.3
  1.1 0.0 copy-done.4
  1.1 0.0 copy-start
  1.1 1.1 %copy-done = bf16[768,512]{1,0:T(8,128)(2,1)S(1)} copy-done((bf16[768,512]{1,0:T(8,128)(2,1)S(1)}, bf16[768,512]{1,0:T(8,128)(2,1)}, u32[]{:S(2)}) %copy-start) | copy-done | bytes 786456
  2.2 39.4 %shard_map.64 = f32[256,512]{1,0:T(8,128)S(1)} custom-call(bf16[768,512]{1,0:T(8,128)(2,1)S(1)} %copy-done, f32[16,9,256]{2,1,0:T(8,128)S(1)} %copy.7.force_ref, f32[1,16,256]{2,1,0:T(8,128)S(1)} %copy-done.1, s32[16,256]{1,0:T(8,128)S(1)} %copy-done.2, s32[1,128]{1,0:T(1,128)S(1)} %bitcast.4, s32[1,128]{1,0:T(1,128)S(1)} %bitcast.5), custom_call_target="tpu_custom_call" | custom-call | tf_op jit(solution)/shard_map/pallas_call | solution.py:272
  41.7 0.8 %multiply_bitcast_fusion = f32[1,256,512]{2,1,0:T(8,128)} fusion(f32[256,512]{1,0:T(8,128)S(1)} %shard_map.64), kind=kLoop, calls=%fused_computation | loop fusion | flops 131072 | bytes 1048576 | tf_op jit(solution)/shard_map/broadcast_in_dim | solution.py:301
Async XLA Ops:
  0.0 1.1 %copy-start.1 = (f32[1,16,256]{2,1,0:T(8,128)S(1)}, f32[1,16,256]{2,1,0:T(8,128)}, u32[]{:S(2)}) copy-start(f32[1,16,256]{2,1,0:T(8,128)} %bond_ref.1) | copy-start | bytes 49156
  0.0 1.1 %copy-start.2 = (s32[16,256]{1,0:T(8,128)S(1)}, s32[16,256]{1,0:T(8,128)}, u32[]{:S(2)}) copy-start(s32[16,256]{1,0:T(8,128)} %nbr_ref.1) | copy-start | bytes 49156
  0.0 1.1 %copy-start.3 = (s32[128]{0:T(128)S(1)}, s32[128]{0:T(128)}, u32[]{:S(2)}) copy-start(s32[128]{0:T(128)} %param.10) | copy-start | bytes 1540
  0.0 1.1 %copy-start.4 = (s32[128]{0:T(128)S(1)}, s32[128]{0:T(128)}, u32[]{:S(2)}) copy-start(s32[128]{0:T(128)} %param.11) | copy-start | bytes 1540
  1.1 1.1 %copy-start = (bf16[768,512]{1,0:T(8,128)(2,1)S(1)}, bf16[768,512]{1,0:T(8,128)(2,1)}, u32[]{:S(2)}) copy-start(bf16[768,512]{1,0:T(8,128)(2,1)} %v_ref.1) | copy-start | bytes 2359300

commit v4 on v3

--- a/solution.py
+++ b/solution.py
@@ -78,8 +78,8 @@
             device_id={"dom": up if side == 0 else down}, device_id_type=MESH)
         for h in range(2) for side in range(2)
     }
-    for copy in halo.values():
-        copy.start()
+    for side in range(2):
+        halo[side, 0].start()
 
     row_of = lax.broadcasted_iota(jnp.int32, (rows, atoms), 0)
     atom_of = lax.broadcasted_iota(jnp.int32, (rows, atoms), 1)
@@ -125,7 +125,12 @@
                     st_lo[at] = (value - high.astype(F32)).astype(BF16)
         return carry
 
-    lax.fori_loop(0, (atoms + 2 * bnd) // group, build, 0)
+    groups = (atoms + 2 * bnd) // group
+    lax.fori_loop(0, groups // 2, build, 0)
+    for side in range(2):
+        halo[side, 0].wait_send()
+        halo[side, 1].start()
+    lax.fori_loop(groups // 2, groups, build, 0)
 
     onward = {}
     tiles_on = []
@@ -189,14 +194,21 @@
             vx[...].reshape(nblk * cols, rows), columns, (((1,), (1,)), ((), ())),
             preferred_element_type=F32)
 
-    def emit(h):
-        for t in range(n - 1):
-            for first, e, make, out, into in ends(t):
-                @pl.when(first == 0)
-                def _(t=t, e=e, make=make, out=out):
+    order = [(t, h) for t in range(n - 1) for h in range(2)]
+
+    def emit(i):
+        t, h = order[i]
+        for way, (first, e, make, out, into) in enumerate(ends(t)):
+            @pl.when(first == 0)
+            def _(way=way, e=e, make=make, out=out):
+                if i >= 2:
+                    t_done, h_done = order[i - 2]
+                    e_done = ends(t_done)[way][1]
                     for r in range(pieces):
-                        out[h, e, r * piece:(r + 1) * piece] = term(h, e, r).astype(out.dtype)
-                        make(h, e, r).start()
+                        make(h_done, e_done, r).wait_send()
+                for r in range(pieces):
+                    out[h, e, r * piece:(r + 1) * piece] = term(h, e, r).astype(out.dtype)
+                    make(h, e, r).start()
 
     own_flux(0)
     pass_halo(0)
@@ -209,10 +221,11 @@
     emit(0)
     pass_halo(1)
     multiply(1, couple(1))
-    emit(1)
-
-    for h in range(2):
-        for t in range(1, n - 1):
+    for i in range(1, len(order)):
+        emit(i)
+
+    for t in range(1, n - 1):
+        for h in range(2):
             for r in range(pieces):
                 for first, e, make, out, into in ends(t):
                     @pl.when((first > 0) & (first <= t))
@@ -244,15 +257,16 @@
                 out_ref[here, there] = (
                     term(h, me, r) + ru[h, me, here].astype(F32) + rd[h, me, here].astype(F32))
 
-    for h in range(2):
-        for t in range(n - 1):
-            for first, e, make, out, into in ends(t):
-                @pl.when(first <= t)
-                def _(e=e, make=make):
-                    for r in range(pieces):
-                        make(h, e, r).wait_send()
-
-    for copy in [*halo.values(), *onward.values(), *tiles, *tiles_on]:
+    for i, (t, h) in enumerate(order):
+        for first, e, make, out, into in ends(t):
+            early = i < len(order) - 2
+
+            @pl.when((first <= t) & (first > 0) if early else first <= t)
+            def _(e=e, make=make):
+                for r in range(pieces):
+                    make(h, e, r).wait_send()
+
+    for copy in [halo[0, 1], halo[1, 1], *onward.values(), *tiles, *tiles_on]:
         copy.wait_send()
 
 

time: 42.7 us -> 40.2 us (0.941)
  Pallas kernels: 39.4 us -> 36.9 us
    pallas_call x1, Pallas kernels: 39.4 us -> 36.9 us  [per_device(): pl.pallas_call(functools.partial(kernel, n, nblk, pieces), out_shape=jax....]
where the time goes in v4:
time: 40.2 us; the launch traced here: 40 us
  Pallas kernels  36.9 us (92%)
  local copies, waits for them, and re-layouts  2.2 us (5%)
  other arithmetic  0.84 us (2%)
    pallas_call x1, Pallas kernels, per_device(): pl.pallas_call(functools.partial(kernel, n, nblk, pieces), out_shape=jax....  36.9 us
    unnamed x11, local copies, waits for them, and re-layouts  2.2 us
    broadcast_in_dim x1, other arithmetic, per_device(): return (result * scale)[None, :, :]  0.84 us

profile of v4, /device:TPU:0, one launch (start us, length us, event | category | flops | bytes accessed | tf_op | source)
XLA Modules:
  0.0 40.0 jit_solution(2724482376945547139)
XLA Ops:
  0.0 0.0 copy-start.1
  0.0 0.0 copy-start.2
  0.0 0.0 copy-start.3
  0.0 0.0 copy-start.4
  0.0 1.1 %copy.7.force_ref = f32[16,9,256]{2,1,0:T(8,128)S(1)} copy(f32[16,9,256]{2,0,1:T(8,128)} %param.7) | data formatting | bytes 294912 | tf_op args[1]
  1.1 0.0 copy-done.1
  1.1 0.0 copy-done.2
  1.1 0.0 copy-done.3
  1.1 0.0 copy-done.4
  1.1 0.0 copy-start
  1.1 1.1 %copy-done = bf16[768,512]{1,0:T(8,128)(2,1)S(1)} copy-done((bf16[768,512]{1,0:T(8,128)(2,1)S(1)}, bf16[768,512]{1,0:T(8,128)(2,1)}, u32[]{:S(2)}) %copy-start) | copy-done | bytes 786456
  2.2 36.9 %shard_map.64 = f32[256,512]{1,0:T(8,128)S(1)} custom-call(bf16[768,512]{1,0:T(8,128)(2,1)S(1)} %copy-done, f32[16,9,256]{2,1,0:T(8,128)S(1)} %copy.7.force_ref, f32[1,16,256]{2,1,0:T(8,128)S(1)} %copy-done.1, s32[16,256]{1,0:T(8,128)S(1)} %copy-done.2, s32[1,128]{1,0:T(1,128)S(1)} %bitcast.4, s32[1,128]{1,0:T(1,128)S(1)} %bitcast.5), custom_call_target="tpu_custom_call" | custom-call | tf_op jit(solution)/shard_map/pallas_call | solution.py:286
  39.2 0.8 %multiply_bitcast_fusion = f32[1,256,512]{2,1,0:T(8,128)} fusion(f32[256,512]{1,0:T(8,128)S(1)} %shard_map.64), kind=kLoop, calls=%fused_computation | loop fusion | flops 131072 | bytes 1048576 | tf_op jit(solution)/shard_map/broadcast_in_dim | solution.py:315
Async XLA Ops:
  0.0 1.1 %copy-start.1 = (f32[1,16,256]{2,1,0:T(8,128)S(1)}, f32[1,16,256]{2,1,0:T(8,128)}, u32[]{:S(2)}) copy-start(f32[1,16,256]{2,1,0:T(8,128)} %bond_ref.1) | copy-start | bytes 49156
  0.0 1.1 %copy-start.2 = (s32[16,256]{1,0:T(8,128)S(1)}, s32[16,256]{1,0:T(8,128)}, u32[]{:S(2)}) copy-start(s32[16,256]{1,0:T(8,128)} %nbr_ref.1) | copy-start | bytes 49156
  0.0 1.1 %copy-start.3 = (s32[128]{0:T(128)S(1)}, s32[128]{0:T(128)}, u32[]{:S(2)}) copy-start(s32[128]{0:T(128)} %param.10) | copy-start | bytes 1540
  0.0 1.1 %copy-start.4 = (s32[128]{0:T(128)S(1)}, s32[128]{0:T(128)}, u32[]{:S(2)}) copy-start(s32[128]{0:T(128)} %param.11) | copy-start | bytes 1540
  1.1 1.1 %copy-start = (bf16[768,512]{1,0:T(8,128)(2,1)S(1)}, bf16[768,512]{1,0:T(8,128)(2,1)}, u32[]{:S(2)}) copy-start(bf16[768,512]{1,0:T(8,128)(2,1)} %v_ref.1) | copy-start | bytes 2359300

commit v5 on v4

--- a/solution.py
+++ b/solution.py
@@ -213,13 +213,13 @@
     own_flux(0)
     pass_halo(0)
     pass_tiles()
-    own_flux(1)
     columns = couple(0)
     for copy in tiles_on:
         copy.wait_recv()
     multiply(0, columns)
     emit(0)
     pass_halo(1)
+    own_flux(1)
     multiply(1, couple(1))
     for i in range(1, len(order)):
         emit(i)

time: 40.2 us -> 40.7 us (1.012)
  Pallas kernels: 36.9 us -> 37.4 us
    pallas_call x1, Pallas kernels: 36.9 us -> 37.4 us  [per_device(): pl.pallas_call(functools.partial(kernel, n, nblk, pieces), out_shape=jax....]
where the time goes in v5:
time: 40.7 us; the launch traced here: 40.5 us
  Pallas kernels  37.4 us (92%)
  local copies, waits for them, and re-layouts  2.2 us (5%)
  other arithmetic  0.84 us (2%)
    pallas_call x1, Pallas kernels, per_device(): pl.pallas_call(functools.partial(kernel, n, nblk, pieces), out_shape=jax....  37.4 us
    unnamed x11, local copies, waits for them, and re-layouts  2.2 us
    broadcast_in_dim x1, other arithmetic, per_device(): return (result * scale)[None, :, :]  0.84 us

profile of v5, /device:TPU:0, one launch (start us, length us, event | category | flops | bytes accessed | tf_op | source)
XLA Modules:
  0.0 40.5 jit_solution(8077180379667270477)
XLA Ops:
  0.0 0.0 copy-start.1
  0.0 0.0 copy-start.2
  0.0 0.0 copy-start.3
  0.0 0.0 copy-start.4
  0.0 1.1 %copy.7.force_ref = f32[16,9,256]{2,1,0:T(8,128)S(1)} copy(f32[16,9,256]{2,0,1:T(8,128)} %param.7) | data formatting | bytes 294912 | tf_op args[1]
  1.1 0.0 copy-done.1
  1.1 0.0 copy-done.2
  1.1 0.0 copy-done.3
  1.1 0.0 copy-done.4
  1.1 0.0 copy-start
  1.1 1.1 %copy-done = bf16[768,512]{1,0:T(8,128)(2,1)S(1)} copy-done((bf16[768,512]{1,0:T(8,128)(2,1)S(1)}, bf16[768,512]{1,0:T(8,128)(2,1)}, u32[]{:S(2)}) %copy-start) | copy-done | bytes 786456
  2.2 37.4 %shard_map.64 = f32[256,512]{1,0:T(8,128)S(1)} custom-call(bf16[768,512]{1,0:T(8,128)(2,1)S(1)} %copy-done, f32[16,9,256]{2,1,0:T(8,128)S(1)} %copy.7.force_ref, f32[1,16,256]{2,1,0:T(8,128)S(1)} %copy-done.1, s32[16,256]{1,0:T(8,128)S(1)} %copy-done.2, s32[1,128]{1,0:T(1,128)S(1)} %bitcast.4, s32[1,128]{1,0:T(1,128)S(1)} %bitcast.5), custom_call_target="tpu_custom_call" | custom-call | tf_op jit(solution)/shard_map/pallas_call | solution.py:286
  39.7 0.8 %multiply_bitcast_fusion = f32[1,256,512]{2,1,0:T(8,128)} fusion(f32[256,512]{1,0:T(8,128)S(1)} %shard_map.64), kind=kLoop, calls=%fused_computation | loop fusion | flops 131072 | bytes 1048576 | tf_op jit(solution)/shard_map/broadcast_in_dim | solution.py:315
Async XLA Ops:
  0.0 1.1 %copy-start.1 = (f32[1,16,256]{2,1,0:T(8,128)S(1)}, f32[1,16,256]{2,1,0:T(8,128)}, u32[]{:S(2)}) copy-start(f32[1,16,256]{2,1,0:T(8,128)} %bond_ref.1) | copy-start | bytes 49156
  0.0 1.1 %copy-start.2 = (s32[16,256]{1,0:T(8,128)S(1)}, s32[16,256]{1,0:T(8,128)}, u32[]{:S(2)}) copy-start(s32[16,256]{1,0:T(8,128)} %nbr_ref.1) | copy-start | bytes 49156
  0.0 1.1 %copy-start.3 = (s32[128]{0:T(128)S(1)}, s32[128]{0:T(128)}, u32[]{:S(2)}) copy-start(s32[128]{0:T(128)} %param.10) | copy-start | bytes 1540
  0.0 1.1 %copy-start.4 = (s32[128]{0:T(128)S(1)}, s32[128]{0:T(128)}, u32[]{:S(2)}) copy-start(s32[128]{0:T(128)} %param.11) | copy-start | bytes 1540
  1.1 1.1 %copy-start = (bf16[768,512]{1,0:T(8,128)(2,1)S(1)}, bf16[768,512]{1,0:T(8,128)(2,1)}, u32[]{:S(2)}) copy-start(bf16[768,512]{1,0:T(8,128)(2,1)} %v_ref.1) | copy-start | bytes 2359300

commit v6 on v4

--- a/solution.py
+++ b/solution.py
@@ -279,7 +279,7 @@
     tile = nblk * cols // n
     wire = BF16 if n <= 4 else F32
     vmem = pl.BlockSpec(memory_space=pltpu.VMEM)
-    pieces = 2
+    pieces = 4 if tile >= 128 else 2
     line = pltpu.VMEM((2, n, tile, half), wire)
     hops = pltpu.SemaphoreType.DMA((2 * n * pieces,))
     dma = pltpu.SemaphoreType.DMA

time: 40.2 us -> 40.8 us (1.015)
  Pallas kernels: 36.9 us -> 37.5 us
    pallas_call x1, Pallas kernels: 36.9 us -> 37.5 us  [per_device(): pl.pallas_call(functools.partial(kernel, n, nblk, pieces), out_shape=jax....]
where the time goes in v6:
time: 40.8 us; the launch traced here: 40.6 us
  Pallas kernels  37.5 us (92%)
  local copies, waits for them, and re-layouts  2.2 us (5%)
  other arithmetic  0.84 us (2%)
    pallas_call x1, Pallas kernels, per_device(): pl.pallas_call(functools.partial(kernel, n, nblk, pieces), out_shape=jax....  37.5 us
    unnamed x11, local copies, waits for them, and re-layouts  2.2 us
    broadcast_in_dim x1, other arithmetic, per_device(): return (result * scale)[None, :, :]  0.84 us

profile of v6, /device:TPU:0, one launch (start us, length us, event | category | flops | bytes accessed | tf_op | source)
XLA Modules:
  0.0 40.6 jit_solution(17626568098531715677)
XLA Ops:
  0.0 0.0 copy-start.1
  0.0 0.0 copy-start.2
  0.0 0.0 copy-start.3
  0.0 0.0 copy-start.4
  0.0 1.1 %copy.7.force_ref = f32[16,9,256]{2,1,0:T(8,128)S(1)} copy(f32[16,9,256]{2,0,1:T(8,128)} %param.7) | data formatting | bytes 294912 | tf_op args[1]
  1.1 0.0 copy-done.1
  1.1 0.0 copy-done.2
  1.1 0.0 copy-done.3
  1.1 0.0 copy-done.4
  1.1 0.0 copy-start
  1.1 1.1 %copy-done = bf16[768,512]{1,0:T(8,128)(2,1)S(1)} copy-done((bf16[768,512]{1,0:T(8,128)(2,1)S(1)}, bf16[768,512]{1,0:T(8,128)(2,1)}, u32[]{:S(2)}) %copy-start) | copy-done | bytes 786456
  2.2 37.5 %shard_map.64 = f32[256,512]{1,0:T(8,128)S(1)} custom-call(bf16[768,512]{1,0:T(8,128)(2,1)S(1)} %copy-done, f32[16,9,256]{2,1,0:T(8,128)S(1)} %copy.7.force_ref, f32[1,16,256]{2,1,0:T(8,128)S(1)} %copy-done.1, s32[16,256]{1,0:T(8,128)S(1)} %copy-done.2, s32[1,128]{1,0:T(1,128)S(1)} %bitcast.4, s32[1,128]{1,0:T(1,128)S(1)} %bitcast.5), custom_call_target="tpu_custom_call" | custom-call | tf_op jit(solution)/shard_map/pallas_call | solution.py:286
  39.8 0.8 %multiply_bitcast_fusion = f32[1,256,512]{2,1,0:T(8,128)} fusion(f32[256,512]{1,0:T(8,128)S(1)} %shard_map.64), kind=kLoop, calls=%fused_computation | loop fusion | flops 131072 | bytes 1048576 | tf_op jit(solution)/shard_map/broadcast_in_dim | solution.py:315
Async XLA Ops:
  0.0 1.1 %copy-start.1 = (f32[1,16,256]{2,1,0:T(8,128)S(1)}, f32[1,16,256]{2,1,0:T(8,128)}, u32[]{:S(2)}) copy-start(f32[1,16,256]{2,1,0:T(8,128)} %bond_ref.1) | copy-start | bytes 49156
  0.0 1.1 %copy-start.2 = (s32[16,256]{1,0:T(8,128)S(1)}, s32[16,256]{1,0:T(8,128)}, u32[]{:S(2)}) copy-start(s32[16,256]{1,0:T(8,128)} %nbr_ref.1) | copy-start | bytes 49156
  0.0 1.1 %copy-start.3 = (s32[128]{0:T(128)S(1)}, s32[128]{0:T(128)}, u32[]{:S(2)}) copy-start(s32[128]{0:T(128)} %param.10) | copy-start | bytes 1540
  0.0 1.1 %copy-start.4 = (s32[128]{0:T(128)S(1)}, s32[128]{0:T(128)}, u32[]{:S(2)}) copy-start(s32[128]{0:T(128)} %param.11) | copy-start | bytes 1540
  1.1 1.1 %copy-start = (bf16[768,512]{1,0:T(8,128)(2,1)S(1)}, bf16[768,512]{1,0:T(8,128)(2,1)}, u32[]{:S(2)}) copy-start(bf16[768,512]{1,0:T(8,128)(2,1)} %v_ref.1) | copy-start | bytes 2359300
